TPU v7x, 128 devices: a whole 4x4x4 slice. The times are simulated.
128 devices in a mesh: req: 8 (over z, core), unit: 16 (over x, y).
Axes of the slice: x: 4, y: 4, z: 4, core: 2. Of those that a mesh axis runs over, the one named last changes fastest.
Arguments:
- tokens: bfloat16 [128, 384, 1536], P('req'), may hold values from -6 to 6
- lengths: int32 [128], P('req'), may hold values from 1 to 384, 30720 in all
- gate_proj: float32 [1536, 3072], P(('req', 'unit')), may hold values from -0.15625 to 0.15625
- input_proj: float32 [1536, 3072], P(('req', 'unit')), may hold values from -0.15625 to 0.15625
- state_proj: float32 [1536, 256], P(('req', 'unit')), may hold values from -0.15625 to 0.15625
- step_proj: float32 [1536, 48], P(('req', 'unit')), may hold values from -0.15625 to 0.15625
- out_proj: float32 [1536, 3072], P(('req', 'unit')), may hold values from -0.109375 to 0.109375
- conv_weight: float32 [4, 3328], replicated, may hold values from -3 to 3
- step_bias: float32 [48], replicated, may hold values from -4 to -1
- log_rate: float32 [48], replicated, may hold values from -3.5 to 0
- skip_gain: float32 [48], replicated, may hold values from 0.5 to 3
- norm_gain: float32 [3072], replicated, may hold values from 0.1 to 1.9
Outputs:
- mixed: bfloat16 [128, 384, 1536], P(('req', 'unit'))
- final_state: float32 [128, 48, 64, 128], P(('req', 'unit'))
All inputs are finite; a program needn't handle non-finite values. No bound on the sum of `lengths` on one device may be relied on, other than what follows from the above.
Results may differ from a plain program's by a relative error of at most 0.0084.
Values may be sent and summed in bfloat16 or wider, within the bound.
No kernel may reach another device: no remote copies, remote signals or barrier semaphores. Data moves between devices by JAX's collectives and lax.ppermute only.
A program may use at most 192 MiB of HBM per device.

v0:
```python
import jax
import jax.numpy as jnp
from jax import lax
from jax.sharding import PartitionSpec as P

SPAN = 128
EPSILON = 1e-05
HIGHEST = lax.Precision.HIGHEST


def causal_conv(values, kernel):
    kernel_len = kernel.shape[0]
    seq_len = values.shape[-2]
    axis_time = values.ndim - 2
    padding = [(0, 0)] * axis_time + [(kernel_len - 1, 0), (0, 0)]
    padded = jnp.pad(values.astype(jnp.float32), padding)
    running = jnp.zeros(values.shape, jnp.float32)
    for offset in range(kernel_len):
        running = running + kernel[offset] * lax.slice_in_dim(
            padded, offset, offset + seq_len, axis=axis_time
        )
    return jax.nn.silu(running)


def ssd_scan(head_in, step_size, b_matrix, c_matrix, rate_per, skip_gain, block_len):
    req_count, seq_len, head_count, head_dim = head_in.shape
    state_dim = b_matrix.shape[-1]
    blocks = seq_len // block_len
    b_short = b_matrix.astype(jnp.bfloat16)
    c_short = c_matrix.astype(jnp.bfloat16)
    b_wide = lax.optimization_barrier(b_short).astype(jnp.float32)
    c_wide = lax.optimization_barrier(c_short).astype(jnp.float32)
    shaped_x = jnp.moveaxis(
        head_in.reshape(req_count, blocks, block_len, head_count, head_dim), 1, 0
    )
    shaped_dt = jnp.moveaxis(step_size.reshape(req_count, blocks, block_len, head_count), 1, 0)
    shaped_bs = jnp.moveaxis(b_short.reshape(req_count, blocks, block_len, state_dim), 1, 0)
    shaped_cs = jnp.moveaxis(c_short.reshape(req_count, blocks, block_len, state_dim), 1, 0)
    shaped_b = jnp.moveaxis(b_wide.reshape(req_count, blocks, block_len, state_dim), 1, 0)
    shaped_c = jnp.moveaxis(c_wide.reshape(req_count, blocks, block_len, state_dim), 1, 0)
    decays = jnp.cumsum(shaped_dt * rate_per, axis=2)
    where_lower = jnp.arange(block_len)[:, None] >= jnp.arange(block_len)[None, :]

    def advance(carried, pieces):
        piece_x, piece_dt, piece_bs, piece_cs, piece_b, piece_c, piece_log = pieces
        intersection = jnp.einsum(
            "rtn,rsn->rts", piece_cs, piece_bs, preferred_element_type=jnp.float32
        )
        log_gaps = piece_log[:, :, None, :] - piece_log[:, None, :, :]
        factor = jnp.exp(jnp.where(where_lower[None, :, :, None], log_gaps, -jnp.inf))
        mixing = intersection[..., None] * factor * piece_dt[:, None, :, :]
        inside = jnp.einsum("rtsh,rshp->rthp", mixing, piece_x, precision=HIGHEST)
        earlier = (
            jnp.einsum("rtn,rhpn->rthp", piece_c, carried, precision=HIGHEST)
            * jnp.exp(piece_log)[..., None]
        )
        ending = piece_log[:, -1, :]
        weight_in = jnp.exp(ending[:, None, :] - piece_log) * piece_dt
        fresh_state = jnp.einsum(
            "rsh,rshp,rsn->rhpn", weight_in, piece_x, piece_b, precision=HIGHEST
        )
        carried = jnp.exp(ending)[:, :, None, None] * carried + fresh_state
        return (carried, inside + earlier)

    start_state = jnp.zeros((req_count, head_count, head_dim, state_dim), jnp.float32)
    final_state, outputs = lax.scan(
        advance,
        start_state,
        (shaped_x, shaped_dt, shaped_bs, shaped_cs, shaped_b, shaped_c, decays),
    )
    scanned = jnp.moveaxis(outputs, 0, 1).reshape(req_count, seq_len, head_count, head_dim)
    return (scanned + skip_gain[:, None] * head_in, final_state)


def body(
    tokens,
    lengths,
    gate_proj,
    input_proj,
    state_proj,
    step_proj,
    out_proj,
    conv_weight,
    step_bias,
    log_rate,
    skip_gain,
    norm_gain,
):
    unit_count = lax.axis_size("unit")
    unit_id = lax.axis_index("unit")
    group_reqs, seq_len, model_dim = tokens.shape
    own_reqs = group_reqs // unit_count
    inner_dim = gate_proj.shape[1]
    head_count = log_rate.shape[0]
    head_dim = inner_dim // head_count
    state_dim = state_proj.shape[1] // 2
    flat_tokens = tokens.reshape(group_reqs * seq_len, model_dim)
    rate_per = -jnp.exp(log_rate)
    position = jnp.arange(seq_len)
    moved = (
        lax.all_to_all(
            gate_proj.astype(jnp.bfloat16), "unit", split_axis=1, concat_axis=0, tiled=True
        ),
        lax.all_to_all(
            input_proj.astype(jnp.bfloat16), "unit", split_axis=1, concat_axis=0, tiled=True
        ),
        lax.all_to_all(
            state_proj.astype(jnp.bfloat16), "unit", split_axis=1, concat_axis=0, tiled=True
        ),
        lax.all_to_all(
            step_proj.astype(jnp.bfloat16), "unit", split_axis=1, concat_axis=0, tiled=True
        ),
        lax.all_to_all(
            out_proj.astype(jnp.bfloat16), "unit", split_axis=1, concat_axis=0, tiled=True
        ),
    )
    pieces = (
        lax.all_gather(moved[0], "req", axis=0, tiled=True),
        lax.all_gather(moved[1], "req", axis=0, tiled=True),
        lax.all_gather(moved[2], "req", axis=0, tiled=True),
        lax.all_gather(moved[3], "req", axis=0, tiled=True),
        lax.all_gather(moved[4], "req", axis=0, tiled=True),
    )
    projected = tuple(
        (
            jnp.dot(flat_tokens, weight_piece, preferred_element_type=jnp.float32)
            for weight_piece in pieces[:4]
        )
    )
    out_piece = pieces[4]
    gate_sum, input_sum, state_sum, step_sum, out_block = projected + (out_piece,)

    def as_cols(summed):
        return summed.astype(jnp.bfloat16).reshape(group_reqs, seq_len, summed.shape[1])

    gate_cols = as_cols(gate_sum)
    input_cols = as_cols(input_sum)
    state_cols = as_cols(state_sum)
    step_cols = as_cols(step_sum)
    own_len = lax.dynamic_slice_in_dim(lengths, unit_id * own_reqs, own_reqs, 0)
    own_live = (position[None, :] < own_len[:, None]).astype(jnp.float32)
    gate_all, input_all, state_all, step_all = (
        lax.all_to_all(gate_cols, "unit", split_axis=0, concat_axis=2, tiled=True),
        lax.all_to_all(input_cols, "unit", split_axis=0, concat_axis=2, tiled=True),
        lax.all_to_all(state_cols, "unit", split_axis=0, concat_axis=2, tiled=True),
        lax.all_to_all(step_cols, "unit", split_axis=0, concat_axis=2, tiled=True),
    )
    x_conv = causal_conv(input_all, conv_weight[:, :inner_dim])
    s_conv = causal_conv(state_all, conv_weight[:, inner_dim:])
    step_size = jax.nn.softplus(step_all.astype(jnp.float32) + step_bias) * own_live[..., None]
    scanned, final_state = ssd_scan(
        x_conv.reshape(own_reqs, seq_len, head_count, head_dim),
        step_size,
        s_conv[..., :state_dim],
        s_conv[..., state_dim:],
        rate_per,
        skip_gain,
        SPAN,
    )
    gated = scanned.reshape(own_reqs, seq_len, inner_dim) * jax.nn.silu(
        gate_all.astype(jnp.float32)
    )
    spread = jnp.mean(gated * gated, axis=-1, keepdims=True)
    normed = (gated * lax.rsqrt(spread + EPSILON) * norm_gain).astype(jnp.bfloat16)
    returned = lax.all_to_all(normed, "unit", split_axis=2, concat_axis=0, tiled=True)
    mixed = lax.psum_scatter(
        jnp.einsum("rse,de->rsd", returned, out_block, preferred_element_type=jnp.float32),
        "unit",
        scatter_dimension=0,
        tiled=True,
    )
    mixed_out = (mixed * own_live[..., None]).astype(jnp.bfloat16)
    return (mixed_out, final_state)


def solution(mesh):
    placed = (
        P("req", None, None),
        P("req"),
        P(("req", "unit"), None),
        P(("req", "unit"), None),
        P(("req", "unit"), None),
        P(("req", "unit"), None),
        P(("req", "unit"), None),
        P(),
        P(),
        P(),
        P(),
        P(),
    )
    return jax.shard_map(
        body,
        mesh=mesh,
        in_specs=placed,
        out_specs=(P(("req", "unit"), None, None), P(("req", "unit"), None, None, None)),
        check_vma=False,
    )
```

profile of v0, /device:TPU:1, one launch (start us, length us, event | category | flops | bytes accessed | tf_op | source)
XLA Modules:
  0.0 799.4 jit_solution(10832921844835051563)
XLA Ops:
  8.6 7.6 all-to-all-start
  34.9 14.1 %all-gather = bf16[8,192,3]{1,2,0:T(4,128)(2,1)S(1)} all-gather(bf16[1,192,3]{1,2,0:T(4,128)(2,1)S(1)} %reshape.481), channel_id=1, replica_groups=mesh['req'=8,'unit'=16] {'req'}, dimensions={0}, use_global_device_ids=true | all-gather | bytes 10368 | tf_op jit(solution)/shard_map/all_gather | solution.py:121
  49.1 12.0 %convolution_convert_fusion.3 = bf16[6144,3]{0,1:T(4,128)(2,1)} fusion(bf16[6144,1536]{1,0:T(8,128)(2,1)} %bitcast.188, bf16[1536,3]{0,1:T(4,128)(2,1)S(1)} %reshape.482), kind=kOutput, calls=%fused_computation.50 | convolution fusion | flops 56641536 | bytes 18920448 | tf_op jit(solution)/shard_map/dot_general | solution.py:126
  61.1 6.9 all-to-all-start.1
  68.2 13.0 %all-gather.1 = bf16[8,192,16]{1,2,0:T(8,128)(2,1)S(1)} all-gather(bf16[1,192,16]{1,2,0:T(8,128)(2,1)S(1)} %reshape.483), channel_id=1, replica_groups=mesh['req'=8,'unit'=16] {'req'}, dimensions={0}, use_global_device_ids=true | all-gather | bytes 55296 | tf_op jit(solution)/shard_map/all_gather | solution.py:120
  81.4 11.3 %convolution_convert_fusion.2 = bf16[6144,16]{0,1:T(8,128)(2,1)S(1)} fusion(bf16[6144,1536]{1,0:T(8,128)(2,1)} %bitcast.189, bf16[1536,16]{0,1:T(8,128)(2,1)S(1)} %reshape.484), kind=kOutput, calls=%fused_computation.49 | convolution fusion | flops 302088192 | bytes 19120128 | tf_op jit(solution)/shard_map/dot_general | solution.py:126
  93.4 6.9 all-to-all-start.2
  110.7 14.9 %all_gather.16 = bf16[1536,192]{1,0:T(8,128)(2,1)S(1)} all-gather(bf16[192,192]{1,0:T(8,128)(2,1)S(1)} %all_to_all.119), channel_id=1, replica_groups=mesh['req'=8,'unit'=16] {'req'}, dimensions={0}, use_global_device_ids=true | all-gather | bytes 663552 | tf_op jit(solution)/shard_map/all_gather | solution.py:119
  125.6 6.9 all-to-all-start.5
  132.6 10.6 %convolution_convert_fusion.1 = bf16[6144,192]{0,1:T(8,128)(2,1)S(1)} fusion(bf16[6144,1536]{1,0:T(8,128)(2,1)} %bitcast.190, bf16[1536,192]{1,0:T(8,128)(2,1)S(1)} %all_gather.16), kind=kOutput, calls=%fused_computation.45 | convolution fusion | flops 3625058304 | bytes 21823488 | tf_op jit(solution)/shard_map/dot_general | solution.py:126
  145.1 6.9 all-to-all-start.3
  152.0 14.2 %all_gather.18 = bf16[1536,192]{1,0:T(8,128)(2,1)S(1)} all-gather(bf16[192,192]{1,0:T(8,128)(2,1)S(1)} %all_to_all.129), channel_id=1, replica_groups=mesh['req'=8,'unit'=16] {'req'}, dimensions={0}, use_global_device_ids=true | all-gather | bytes 663552 | tf_op jit(solution)/shard_map/all_gather | solution.py:118
  166.2 10.6 %convolution_convert_fusion = bf16[6144,192]{0,1:T(8,128)(2,1)S(1)} fusion(bf16[6144,1536]{1,0:T(8,128)(2,1)} %bitcast.191, bf16[1536,192]{1,0:T(8,128)(2,1)S(1)} %all_gather.18), kind=kOutput, calls=%fused_computation.44 | convolution fusion | flops 3625058304 | bytes 21823488 | tf_op jit(solution)/shard_map/dot_general | solution.py:126
  192.8 6.9 divide_multiply_fusion
  199.6 8.0 transpose_reshape_reshape.3
  207.6 173.0 %while.13 = (s32[]{:T(128)}, f32[1,48,64,128]{3,2,1,0:T(8,128)S(1)}, f32[3,1,128,48,64]{2,0,4,3,1:T(4,128)}, f32[3,1,128,48]{2,3,1,0:T(8,128)S(1)}, f32[3,1,128,...) while((s32[]{:T(128)}, ...), condition=%wide.region_2.3_spmd.clone, body=%wide.region_1.2_spmd.clone.sunk | while | flops 1822060544 | bytes 19582040 | solution.py:66
  216.3 7.4 bitcast_add_fusion.5
  223.7 39.1 %dynamic_update_slice.6 = f32[3,1,128,48,64]{2,0,4,3,1:T(4,128)} dynamic-update-slice(f32[3,1,128,48,64]{2,0,4,3,1:T(4,128)} %get-tuple-element.262, f32[1,1,128,48,64]{2,0,4,3,1:T(1,128)} %bitcast.194, s32[]{:T(128)} %get-tuple-element.260, s32[]{:T(128)} %constant.43.clone.1..sunk, s32[]{:T(128)} %constant.43.clone.1..sunk, s32[]{:T(128)} %constant.43.clone.1..sunk, s32[]{:T(128)} %constant.43.clone.1..sunk) | dynamic-update-slice | bytes 3145732 | tf_op jit(solution)/shard_map/while/body/jit(dynamic_update_index_in_dim)/dynamic_update_slice | solution.py:66
  274.0 7.4 bitcast_add_fusion.5
  281.3 39.1 %dynamic_update_slice.6 = f32[3,1,128,48,64]{2,0,4,3,1:T(4,128)} dynamic-update-slice(f32[3,1,128,48,64]{2,0,4,3,1:T(4,128)} %get-tuple-element.262, f32[1,1,128,48,64]{2,0,4,3,1:T(1,128)} %bitcast.194, s32[]{:T(128)} %get-tuple-element.260, s32[]{:T(128)} %constant.43.clone.1..sunk, s32[]{:T(128)} %constant.43.clone.1..sunk, s32[]{:T(128)} %constant.43.clone.1..sunk, s32[]{:T(128)} %constant.43.clone.1..sunk) | dynamic-update-slice | bytes 3145732 | tf_op jit(solution)/shard_map/while/body/jit(dynamic_update_index_in_dim)/dynamic_update_slice | solution.py:66
  331.6 7.4 bitcast_add_fusion.5
  339.0 39.1 %dynamic_update_slice.6 = f32[3,1,128,48,64]{2,0,4,3,1:T(4,128)} dynamic-update-slice(f32[3,1,128,48,64]{2,0,4,3,1:T(4,128)} %get-tuple-element.262, f32[1,1,128,48,64]{2,0,4,3,1:T(1,128)} %bitcast.194, s32[]{:T(128)} %get-tuple-element.260, s32[]{:T(128)} %constant.43.clone.1..sunk, s32[]{:T(128)} %constant.43.clone.1..sunk, s32[]{:T(128)} %constant.43.clone.1..sunk, s32[]{:T(128)} %constant.43.clone.1..sunk) | dynamic-update-slice | bytes 3145732 | tf_op jit(solution)/shard_map/while/body/jit(dynamic_update_index_in_dim)/dynamic_update_slice | solution.py:66
  380.6 9.1 %reshape_transpose.3 = f32[1,384,3072]{1,2,0:T(8,128)} reshape(f32[3,1,128,48,64]{2,0,4,3,1:T(4,128)} %get-tuple-element.60) | data formatting | bytes 9437184 | tf_op jit(solution)/shard_map/reshape;transpose | solution.py:71
  389.7 6.8 all-to-all-start.9
  396.5 15.3 %multiply_reduce_fusion = (f32[384]{0:T(512)S(1)}, f32[1,384,3072]{1,2,0:T(8,128)S(1)}) fusion(bf16[16,384,192]{1,2,0:T(8,128)(2,1)} %all-to-all-done.7, f32[1,384,3072]{1,2,0:T(8,128)} %reshape_transpose.3, f32[3072]{0:T(1024)S(1)} %mul.288, f32[1,384,3072]{1,2,0:T(8,128)} %bitcast.193, f32[3072]{0:T(1024)S(1)} %bitcast.216, f32[3072]{0:T(1024)S(1)} %bitcast.218, ...), kind=kLoop, calls=%fused_computation.64 | loop fusion | flops 24772224 | bytes 16578048 | tf_op jit(solution)/shard_map/reduce_sum | solution.py:163
  412.4 44.7 %copy.164 = bf16[1,384,3072]{1,0,2:T(2,128)(2,1)} copy(bf16[1,384,3072]{1,2,0:T(8,128)(2,1)S(1)} %multiply_convert_fusion) | data formatting | bytes 4718592 | tf_op jit(solution)/shard_map/convert_element_type | solution.py:164
  457.6 50.9 %reduce.4 = bf16[3072,384]{1,0:T(8,128)(2,1)S(1)} reduce(bf16[3072,1,384]{2,1,0:T(2,128)(2,1)} %bitcast.195, bf16[]{:T(256)} %broadcast.240), dimensions={1}, to_apply=%bitcast.159.reduce_sub_computation | reduce | bytes 4718594
  517.5 16.9 %all_gather.19 = bf16[1536,192]{1,0:T(8,128)(2,1)S(1)} all-gather(bf16[192,192]{1,0:T(8,128)(2,1)S(1)} %all_to_all.138), channel_id=1, replica_groups=mesh['req'=8,'unit'=16] {'req'}, dimensions={0}, use_global_device_ids=true | all-gather | bytes 663552 | tf_op jit(solution)/shard_map/all_gather | solution.py:122
  534.4 10.7 %all-to-all-done.8 = bf16[16,2,36864]{2,1,0:T(2,128)(2,1)S(1)} async-done(((bf16[16,2,36864]{2,1,0:T(2,128)(2,1)}), bf16[16,2,36864]{2,1,0:T(2,128)(2,1)S(1)}, u32[]{:S(2)}, u32[]{:S(2)}) %all-to-all-start.8) | async-done | bytes 2359328 | tf_op jit(solution)/shard_map/all_to_all | solution.py:165
  545.1 6.9 reshape.501
  554.8 14.9 %fusion.50 = f32[16,384,1536]{2,1,0:T(8,128)} fusion(bf16[16,384,192]{1,2,0:T(8,128)(2,1)S(1)} %bitcast.197, bf16[1536,192]{1,0:T(8,128)(2,1)S(1)} %all_gather.19), kind=kOutput, calls=%fused_computation.70 | convolution fusion | flops 3623878656 | bytes 40697856 | tf_op jit(solution)/shard_map/rse,de->rsd/dot_general | solution.py:167
  570.3 219.0 %reduce-scatter.4.cloned.1.call-done = f32[1,384,1536]{2,1,0:T(8,128)} async-done(((f32[16,384,1536]{2,1,0:T(8,128)}), f32[1,384,1536]{2,1,0:T(8,128)}) %reduce-scatter.4.cloned.1.call-update) | async-done | bytes 2359312
  (115 shorter events, 98.9 us)
Async XLA Ops:
  8.6 19.6 %all-to-all-start = ((bf16[12,16,3]{0,2,1:T(4,128)(2,1)}), bf16[12,16,3]{0,2,1:T(4,128)(2,1)S(1)}, u32[]{:S(2)}, u32[]{:S(2)}) async-start(bf16[12,16,3]{0,2,1:T(4,128)(2,1)} %all_to_all.111), calls=%async_computation | async-start | bytes 32768 | tf_op jit(solution)/shard_map/all_to_all | solution.py:110
  28.2 32.9 %all-to-all-start.4 = ((bf16[12,16,16]{0,2,1:T(8,128)(2,1)}), bf16[12,16,16]{0,2,1:T(8,128)(2,1)S(1)}, u32[]{:S(2)}, u32[]{:S(2)}) async-start(bf16[12,16,16]{0,2,1:T(8,128)(2,1)} %bitcast.17), calls=%async_computation.4 | async-start | bytes 131072 | tf_op jit(solution)/shard_map/all_to_all | solution.py:107
  61.1 32.3 %all-to-all-start.1 = ((bf16[16,384,3]{1,2,0:T(4,128)(2,1)}), bf16[16,384,3]{1,2,0:T(4,128)(2,1)S(1)}, u32[]{:S(2)}, u32[]{:S(2)}) async-start(bf16[16,384,3]{1,2,0:T(4,128)(2,1)} %bitcast.2), calls=%async_computation.1 | async-start | bytes 98304 | tf_op jit(solution)/shard_map/all_to_all | solution.py:146
  81.4 19.1 %copy-start.3 = (f32[48]{0:T(128)S(1)}, f32[48]{0:T(128)}, u32[]{:S(2)}) copy-start(f32[48]{0:T(128)} %param.22) | copy-start | bytes 580
  93.4 13.7 %all-to-all-start.2 = ((bf16[12,16,192]{2,0,1:T(8,128)(2,1)}), bf16[12,16,192]{2,0,1:T(8,128)(2,1)S(1)}, u32[]{:S(2)}, u32[]{:S(2)}) async-start(bf16[12,16,192]{2,0,1:T(8,128)(2,1)} %copy.121), calls=%async_computation.2 | async-start | bytes 262144 | tf_op jit(solution)/shard_map/all_to_all | solution.py:104
  107.1 18.5 %all-to-all-start.6 = ((bf16[12,16,192]{2,0,1:T(8,128)(2,1)}), bf16[12,16,192]{2,0,1:T(8,128)(2,1)S(1)}, u32[]{:S(2)}, u32[]{:S(2)}) async-start(bf16[12,16,192]{2,0,1:T(8,128)(2,1)} %copy.139), calls=%async_computation.6 | async-start | bytes 262144 | tf_op jit(solution)/shard_map/all_to_all | solution.py:101
  125.6 19.4 %all-to-all-start.5 = ((bf16[16,384,16]{1,2,0:T(8,128)(2,1)}), bf16[16,384,16]{1,2,0:T(8,128)(2,1)S(1)}, u32[]{:S(2)}, u32[]{:S(2)}) async-start(bf16[16,384,16]{1,2,0:T(8,128)(2,1)} %bitcast.158), calls=%async_computation.5 | async-start | bytes 393216 | tf_op jit(solution)/shard_map/all_to_all | solution.py:145
  145.1 38.5 %all-to-all-start.3 = ((bf16[16,384,192]{1,2,0:T(8,128)(2,1)}), bf16[16,384,192]{1,2,0:T(8,128)(2,1)}, u32[]{:S(2)}, u32[]{:S(2)}) async-start(bf16[16,384,192]{1,2,0:T(8,128)(2,1)} %bitcast.199), calls=%async_computation.3 | async-start | bytes 4718592 | tf_op jit(solution)/shard_map/all_to_all | solution.py:144
  183.6 206.1 %all-to-all-start.7 = ((bf16[16,384,192]{1,2,0:T(8,128)(2,1)}), bf16[16,384,192]{1,2,0:T(8,128)(2,1)}, u32[]{:S(2)}, u32[]{:S(2)}) async-start(bf16[16,384,192]{1,2,0:T(8,128)(2,1)} %bitcast.198), calls=%async_computation.7 | async-start | bytes 4718592 | tf_op jit(solution)/shard_map/all_to_all | solution.py:143
  190.7 2.1 copy-start.1
  380.6 9.1 %copy-start = (f32[1,48,64,128]{3,2,1,0:T(8,128)}, f32[1,48,64,128]{3,2,1,0:T(8,128)S(1)}, u32[]{:S(2)}) copy-start(f32[1,48,64,128]{3,2,1,0:T(8,128)S(1)} %get-tuple-element.59) | copy-start | bytes 4718596
  389.7 120.9 %all-to-all-start.9 = ((bf16[12,16,192]{2,0,1:T(8,128)(2,1)}), bf16[12,16,192]{2,0,1:T(8,128)(2,1)S(1)}, u32[]{:S(2)}, u32[]{:S(2)}) async-start(bf16[12,16,192]{2,0,1:T(8,128)(2,1)} %copy.142), calls=%async_computation.9 | async-start | bytes 262144 | tf_op jit(solution)/shard_map/all_to_all | solution.py:113
  396.5 15.3 %copy-start.2 = (f32[3072]{0:T(1024)S(1)}, f32[3072]{0:T(1024)}, u32[]{:S(2)}) copy-start(f32[3072]{0:T(1024)} %param.25) | copy-start | bytes 36868
  510.6 34.5 %all-to-all-start.8 = ((bf16[16,2,36864]{2,1,0:T(2,128)(2,1)}), bf16[16,2,36864]{2,1,0:T(2,128)(2,1)S(1)}, u32[]{:S(2)}, u32[]{:S(2)}) async-start(bf16[16,2,36864]{2,1,0:T(2,128)(2,1)} %reshape.500), calls=%async_computation.8 | async-start | bytes 4718592 | tf_op jit(solution)/shard_map/all_to_all | solution.py:165
  517.4 271.9 %reduce-scatter.4.cloned.1.call-start = ((), (), s32[]{:S(2)}) async-start(), calls=%async_computation.11 | async-start | bytes 40108032
Sparse Core Ops, SparseCore 0:
  569.9 219.3 reduce-scatter.3
where the time goes:
time: 813 us; the launch traced here: 799 us
  waiting for transfers between devices  237 us (29%)
  local copies, waits for them, and re-layouts  226 us (28%)
  matrix products  97.7 us (12%)
  other arithmetic  86.6 us (11%)
  blocking collectives  73.2 us (9%)
  starting transfers between devices  64 us (8%)
  between operations  14.8 us (2%)
    unnamed x2, waiting for transfers between devices  219 us
    dynamic_update_slice x3, local copies, waits for them, and re-layouts, ssd_scan(): lax.scan(advance, start_state, (shaped_x, shaped_dt, shaped_bs, shaped_cs...  117 us
    unnamed x2, other arithmetic  50.9 us
    convert_element_type x1, local copies, waits for them, and re-layouts, body(): (gated * lax.rsqrt(spread + EPSILON) * norm_gain).astype(jnp.bfloat16)  44.7 us
    dot_general x4, matrix products, body(): jnp.dot(flat_tokens, weight_piece, preferred_element_type=jnp.float32)  44.5 us
    dot_general x3, matrix products, advance(): inside = jnp.einsum('rtsh,rshp->rthp', mixing, piece_x, precision=HIGHEST)  22.1 us
    all_gather x1, blocking collectives, body(): lax.all_gather(moved[4], 'req', axis=0, tiled=True)  16.9 us
  transfers between devices with their start and end apart: 11, of which 4 were waited for; matrix products, arithmetic and copies ran while one was open for 47% of the time, Pallas kernels for 0%

commit v1 on v0

--- a/solution.py
+++ b/solution.py
@@ -162,7 +162,10 @@
     )
     spread = jnp.mean(gated * gated, axis=-1, keepdims=True)
     normed = (gated * lax.rsqrt(spread + EPSILON) * norm_gain).astype(jnp.bfloat16)
-    returned = lax.all_to_all(normed, "unit", split_axis=2, concat_axis=0, tiled=True)
+    returned = jnp.concatenate(
+        lax.all_to_all(jnp.stack(jnp.split(normed, lax.axis_size("unit"), axis=2)), "unit", 0, 0),
+        axis=0,
+    )
     mixed = lax.psum_scatter(
         jnp.einsum("rse,de->rsd", returned, out_block, preferred_element_type=jnp.float32),
         "unit",

time: 813 us -> 729 us (0.90)
  other arithmetic: 86.6 us -> 35.9 us
  local copies, waits for them, and re-layouts: 226 us -> 180 us
  starting transfers between devices: 64 us -> 75.7 us
    unnamed x2 -> x1, other arithmetic: 50.9 us -> 0.01 us
    convert_element_type x1 -> x0, local copies, waits for them, and re-layouts: 44.7 us -> none  [body(): (gated * lax.rsqrt(spread + EPSILON) * norm_gain).astype(jnp.bfloat16)]
    all_to_all x1, starting transfers between devices: 6.88 us -> 19 us  [body(): lax.all_to_all(input_cols, 'unit', split_axis=0, concat_axis=2, tiled=True)]
  transfers between devices with their start and end apart: 11 -> 11, of which waited for: 4 -> 4; matrix products, arithmetic and copies ran while one was open for 47% -> 41% of each run, Pallas kernels for 0% -> 0%
where the time goes in v1:
time: 729 us; the launch traced here: 716 us
  waiting for transfers between devices  237 us (33%)
  local copies, waits for them, and re-layouts  180 us (25%)
  matrix products  99.1 us (14%)
  starting transfers between devices  75.7 us (10%)
  blocking collectives  73.3 us (10%)
  other arithmetic  35.9 us (5%)
  between operations  14.7 us (2%)
    unnamed x2, waiting for transfers between devices  219 us
    dynamic_update_slice x3, local copies, waits for them, and re-layouts, ssd_scan(): lax.scan(advance, start_state, (shaped_x, shaped_dt, shaped_bs, shaped_cs...  117 us
    dot_general x4, matrix products, body(): jnp.dot(flat_tokens, weight_piece, preferred_element_type=jnp.float32)  44.2 us
    dot_general x3, matrix products, advance(): inside = jnp.einsum('rtsh,rshp->rthp', mixing, piece_x, precision=HIGHEST)  22.1 us
    all_to_all x1, starting transfers between devices, body(): lax.all_to_all(input_cols, 'unit', split_axis=0, concat_axis=2, tiled=True)  19 us
    all_gather x1, blocking collectives, body(): lax.all_gather(moved[4], 'req', axis=0, tiled=True)  17 us
    dot_general x1, matrix products, body(): jnp.einsum('rse,de->rsd', returned, out_block, preferred_element_type=jnp...  16.6 us
    dynamic_slice x6, local copies, waits for them, and re-layouts, ssd_scan(): lax.scan(advance, start_state, (shaped_x, shaped_dt, shaped_bs, shaped_cs...  16.2 us
  transfers between devices with their start and end apart: 11, of which 4 were waited for; matrix products, arithmetic and copies ran while one was open for 41% of the time, Pallas kernels for 0%

profile of v1, /device:TPU:1, one launch (start us, length us, event | category | flops | bytes accessed | tf_op | source)
XLA Modules:
  0.0 715.7 jit_solution(15686566084161690954)
XLA Ops:
  8.6 7.6 %all-to-all-start = ((bf16[12,16,3]{0,2,1:T(4,128)(2,1)}), bf16[12,16,3]{0,2,1:T(4,128)(2,1)S(1)}, u32[]{:S(2)}, u32[]{:S(2)}) async-start(bf16[12,16,3]{0,2,1:T(4,128)(2,1)} %all_to_all.101), calls=%async_computation | async-start | bytes 32768 | tf_op jit(solution)/shard_map/all_to_all | solution.py:110
  28.3 6.7 all-to-all-start.4
  35.0 14.1 %all-gather = bf16[8,192,3]{1,2,0:T(4,128)(2,1)S(1)} all-gather(bf16[1,192,3]{1,2,0:T(4,128)(2,1)S(1)} %reshape.485), channel_id=1, replica_groups=mesh['req'=8,'unit'=16] {'req'}, dimensions={0}, use_global_device_ids=true | all-gather | bytes 10368 | tf_op jit(solution)/shard_map/all_gather | solution.py:121
  49.2 12.0 %convolution_convert_fusion.3 = bf16[6144,3]{0,1:T(4,128)(2,1)} fusion(bf16[6144,1536]{1,0:T(8,128)(2,1)} %bitcast.245, bf16[1536,3]{0,1:T(4,128)(2,1)S(1)} %reshape.486), kind=kOutput, calls=%fused_computation.50 | convolution fusion | flops 56641536 | bytes 18920448 | tf_op jit(solution)/shard_map/dot_general | solution.py:126
  61.2 6.9 all-to-all-start.1
  68.3 13.0 %all-gather.1 = bf16[8,192,16]{1,2,0:T(8,128)(2,1)S(1)} all-gather(bf16[1,192,16]{1,2,0:T(8,128)(2,1)S(1)} %reshape.487), channel_id=1, replica_groups=mesh['req'=8,'unit'=16] {'req'}, dimensions={0}, use_global_device_ids=true | all-gather | bytes 55296 | tf_op jit(solution)/shard_map/all_gather | solution.py:120
  81.5 11.3 %convolution_convert_fusion.2 = bf16[6144,16]{0,1:T(8,128)(2,1)S(1)} fusion(bf16[6144,1536]{1,0:T(8,128)(2,1)} %bitcast.246, bf16[1536,16]{0,1:T(8,128)(2,1)S(1)} %reshape.488), kind=kOutput, calls=%fused_computation.49 | convolution fusion | flops 302088192 | bytes 19120128 | tf_op jit(solution)/shard_map/dot_general | solution.py:126
  93.5 6.9 all-to-all-start.2
  101.9 5.3 all-to-all-done.2
  110.8 14.9 %all_gather.16 = bf16[1536,192]{1,0:T(8,128)(2,1)S(1)} all-gather(bf16[192,192]{1,0:T(8,128)(2,1)S(1)} %all_to_all.109), channel_id=1, replica_groups=mesh['req'=8,'unit'=16] {'req'}, dimensions={0}, use_global_device_ids=true | all-gather | bytes 663552 | tf_op jit(solution)/shard_map/all_gather | solution.py:119
  125.8 6.9 all-to-all-start.5
  132.7 10.5 %convolution_convert_fusion.1 = bf16[6144,192]{0,1:T(8,128)(2,1)S(1)} fusion(bf16[6144,1536]{1,0:T(8,128)(2,1)} %bitcast.247, bf16[1536,192]{1,0:T(8,128)(2,1)S(1)} %all_gather.16), kind=kOutput, calls=%fused_computation.45 | convolution fusion | flops 3625058304 | bytes 21823488 | tf_op jit(solution)/shard_map/dot_general | solution.py:126
  145.1 19.0 %all-to-all-start.3 = ((bf16[16,384,192]{1,2,0:T(8,128)(2,1)}), bf16[16,384,192]{1,2,0:T(8,128)(2,1)}, u32[]{:S(2)}, u32[]{:S(2)}) async-start(bf16[16,384,192]{1,2,0:T(8,128)(2,1)} %bitcast.253), calls=%async_computation.3 | async-start | bytes 4718592 | tf_op jit(solution)/shard_map/all_to_all | solution.py:144
  164.1 14.2 %all_gather.18 = bf16[1536,192]{1,0:T(8,128)(2,1)S(1)} all-gather(bf16[192,192]{1,0:T(8,128)(2,1)S(1)} %all_to_all.119), channel_id=1, replica_groups=mesh['req'=8,'unit'=16] {'req'}, dimensions={0}, use_global_device_ids=true | all-gather | bytes 663552 | tf_op jit(solution)/shard_map/all_gather | solution.py:118
  178.3 10.5 %convolution_convert_fusion = bf16[6144,192]{0,1:T(8,128)(2,1)S(1)} fusion(bf16[6144,1536]{1,0:T(8,128)(2,1)} %bitcast.248, bf16[1536,192]{1,0:T(8,128)(2,1)S(1)} %all_gather.18), kind=kOutput, calls=%fused_computation.44 | convolution fusion | flops 3625058304 | bytes 21823488 | tf_op jit(solution)/shard_map/dot_general | solution.py:126
  204.7 6.9 divide_multiply_fusion
  211.6 8.0 %transpose_reshape_reshape.3 = f32[3,1,128,48,64]{2,0,4,3,1:T(4,128)} reshape(f32[1,384,3072]{1,2,0:T(8,128)} %divide_multiply_fusion) | data formatting | bytes 9437184 | tf_op jit(solution)/shard_map/transpose;reshape;reshape | solution.py:33
  219.6 173.0 %while.13 = (s32[]{:T(128)}, f32[1,48,64,128]{3,2,1,0:T(8,128)S(1)}, f32[3,1,128,48,64]{2,0,4,3,1:T(4,128)}, f32[3,1,128,48]{2,3,1,0:T(8,128)S(1)}, f32[3,1,128,...) while((s32[]{:T(128)}, ...), condition=%wide.region_2.3_spmd.clone, body=%wide.region_1.2_spmd.clone.sunk | while | flops 1822060544 | bytes 19582040 | solution.py:66
  228.3 7.4 %bitcast_add_fusion.5 = f32[1,128,48,64]{1,3,2,0:T(8,128)} fusion(f32[128,48,64]{0,2,1:T(8,128)S(1)} %fusion.113, f32[128,48,64]{0,2,1:T(8,128)S(1)} %bitcast.243, f32[128,48]{0,1:T(8,128)S(1)} %bitcast.254, f32[128,48]{0,1:T(8,128)S(1)} %get-tuple-element.246, f32[128,128]{1,0:T(8,128)S(1)} %fusion.114, ...), kind=kOutput, calls=%fused_computation.7.clone.1 | convolution fusion | flops 607911936 | bytes 4874240 | tf_op jit(solution)/shard_map/while/body/eval_jaxpr/rtsh,rshp->rthp/dot_general | solution.py:52
  235.7 39.1 %dynamic_update_slice.6 = f32[3,1,128,48,64]{2,0,4,3,1:T(4,128)} dynamic-update-slice(f32[3,1,128,48,64]{2,0,4,3,1:T(4,128)} %get-tuple-element.262, f32[1,1,128,48,64]{2,0,4,3,1:T(1,128)} %bitcast.251, s32[]{:T(128)} %get-tuple-element.260, s32[]{:T(128)} %constant.43.clone.1..sunk, s32[]{:T(128)} %constant.43.clone.1..sunk, s32[]{:T(128)} %constant.43.clone.1..sunk, s32[]{:T(128)} %constant.43.clone.1..sunk) | dynamic-update-slice | bytes 3145732 | tf_op jit(solution)/shard_map/while/body/jit(dynamic_update_index_in_dim)/dynamic_update_slice | solution.py:66
  286.0 7.4 %bitcast_add_fusion.5 = f32[1,128,48,64]{1,3,2,0:T(8,128)} fusion(f32[128,48,64]{0,2,1:T(8,128)S(1)} %fusion.113, f32[128,48,64]{0,2,1:T(8,128)S(1)} %bitcast.243, f32[128,48]{0,1:T(8,128)S(1)} %bitcast.254, f32[128,48]{0,1:T(8,128)S(1)} %get-tuple-element.246, f32[128,128]{1,0:T(8,128)S(1)} %fusion.114, ...), kind=kOutput, calls=%fused_computation.7.clone.1 | convolution fusion | flops 607911936 | bytes 4874240 | tf_op jit(solution)/shard_map/while/body/eval_jaxpr/rtsh,rshp->rthp/dot_general | solution.py:52
  293.3 39.1 %dynamic_update_slice.6 = f32[3,1,128,48,64]{2,0,4,3,1:T(4,128)} dynamic-update-slice(f32[3,1,128,48,64]{2,0,4,3,1:T(4,128)} %get-tuple-element.262, f32[1,1,128,48,64]{2,0,4,3,1:T(1,128)} %bitcast.251, s32[]{:T(128)} %get-tuple-element.260, s32[]{:T(128)} %constant.43.clone.1..sunk, s32[]{:T(128)} %constant.43.clone.1..sunk, s32[]{:T(128)} %constant.43.clone.1..sunk, s32[]{:T(128)} %constant.43.clone.1..sunk) | dynamic-update-slice | bytes 3145732 | tf_op jit(solution)/shard_map/while/body/jit(dynamic_update_index_in_dim)/dynamic_update_slice | solution.py:66
  343.6 7.4 %bitcast_add_fusion.5 = f32[1,128,48,64]{1,3,2,0:T(8,128)} fusion(f32[128,48,64]{0,2,1:T(8,128)S(1)} %fusion.113, f32[128,48,64]{0,2,1:T(8,128)S(1)} %bitcast.243, f32[128,48]{0,1:T(8,128)S(1)} %bitcast.254, f32[128,48]{0,1:T(8,128)S(1)} %get-tuple-element.246, f32[128,128]{1,0:T(8,128)S(1)} %fusion.114, ...), kind=kOutput, calls=%fused_computation.7.clone.1 | convolution fusion | flops 607911936 | bytes 4874240 | tf_op jit(solution)/shard_map/while/body/eval_jaxpr/rtsh,rshp->rthp/dot_general | solution.py:52
  351.0 39.1 %dynamic_update_slice.6 = f32[3,1,128,48,64]{2,0,4,3,1:T(4,128)} dynamic-update-slice(f32[3,1,128,48,64]{2,0,4,3,1:T(4,128)} %get-tuple-element.262, f32[1,1,128,48,64]{2,0,4,3,1:T(1,128)} %bitcast.251, s32[]{:T(128)} %get-tuple-element.260, s32[]{:T(128)} %constant.43.clone.1..sunk, s32[]{:T(128)} %constant.43.clone.1..sunk, s32[]{:T(128)} %constant.43.clone.1..sunk, s32[]{:T(128)} %constant.43.clone.1..sunk) | dynamic-update-slice | bytes 3145732 | tf_op jit(solution)/shard_map/while/body/jit(dynamic_update_index_in_dim)/dynamic_update_slice | solution.py:66
  392.6 9.1 %reshape_transpose.3 = f32[1,384,3072]{1,2,0:T(8,128)} reshape(f32[3,1,128,48,64]{2,0,4,3,1:T(4,128)} %get-tuple-element.60) | data formatting | bytes 9437184 | tf_op jit(solution)/shard_map/reshape;transpose | solution.py:71
  401.7 6.6 all-to-all-start.9
  408.4 15.3 %multiply_reduce_fusion = (f32[384]{0:T(512)S(1)}, f32[1,384,3072]{1,2,0:T(8,128)S(1)}) fusion(bf16[16,384,192]{1,2,0:T(8,128)(2,1)} %all-to-all-done.7, f32[1,384,3072]{1,2,0:T(8,128)} %reshape_transpose.3, f32[3072]{0:T(1024)S(1)} %mul.288, f32[1,384,3072]{1,2,0:T(8,128)} %bitcast.250, f32[3072]{0:T(1024)S(1)} %bitcast.270, f32[3072]{0:T(1024)S(1)} %bitcast.272, ...), kind=kLoop, calls=%fused_computation.64 | loop fusion | flops 24772224 | bytes 16578048 | tf_op jit(solution)/shard_map/reduce_sum | solution.py:163
  435.0 6.7 all-to-all-start.8
  441.8 17.0 %all_gather.19 = bf16[1536,192]{1,0:T(8,128)(2,1)S(1)} all-gather(bf16[192,192]{1,0:T(8,128)(2,1)S(1)} %all_to_all.125), channel_id=1, replica_groups=mesh['req'=8,'unit'=16] {'req'}, dimensions={0}, use_global_device_ids=true | all-gather | bytes 663552 | tf_op jit(solution)/shard_map/all_gather | solution.py:122
  458.8 10.6 %all-to-all-done.8 = bf16[16,1,384,192]{2,3,1,0:T(8,128)(2,1)} async-done(((bf16[16,1,384,192]{2,3,1,0:T(8,128)(2,1)}), bf16[16,1,384,192]{2,3,1,0:T(8,128)(2,1)}, u32[]{:S(2)}, u32[]{:S(2)}) %all-to-all-start.8) | async-done | bytes 2359328 | tf_op jit(solution)/shard_map/all_to_all | solution.py:166
  469.4 16.6 %fusion.50 = f32[16,384,1536]{2,1,0:T(8,128)} fusion(bf16[16,1,384,192]{2,3,1,0:T(8,128)(2,1)} %all-to-all-done.8, bf16[1536,192]{1,0:T(8,128)(2,1)S(1)} %all_gather.19), kind=kOutput, calls=%fused_computation.68 | convolution fusion | flops 3623878656 | bytes 40697856 | tf_op jit(solution)/shard_map/rse,de->rsd/dot_general | solution.py:170
  486.7 219.0 %reduce-scatter.4.cloned.1.call-done = f32[1,384,1536]{2,1,0:T(8,128)} async-done(((f32[16,384,1536]{2,1,0:T(8,128)}), f32[1,384,1536]{2,1,0:T(8,128)}) %reduce-scatter.4.cloned.1.call-update) | async-done | bytes 2359312
  (125 shorter events, 85.7 us)
Async XLA Ops:
  8.6 19.7 %all-to-all-start = ((bf16[12,16,3]{0,2,1:T(4,128)(2,1)}), bf16[12,16,3]{0,2,1:T(4,128)(2,1)S(1)}, u32[]{:S(2)}, u32[]{:S(2)}) async-start(bf16[12,16,3]{0,2,1:T(4,128)(2,1)} %all_to_all.101), calls=%async_computation | async-start | bytes 32768 | tf_op jit(solution)/shard_map/all_to_all | solution.py:110
  28.3 32.9 %all-to-all-start.4 = ((bf16[12,16,16]{0,2,1:T(8,128)(2,1)}), bf16[12,16,16]{0,2,1:T(8,128)(2,1)S(1)}, u32[]{:S(2)}, u32[]{:S(2)}) async-start(bf16[12,16,16]{0,2,1:T(8,128)(2,1)} %bitcast.17), calls=%async_computation.4 | async-start | bytes 131072 | tf_op jit(solution)/shard_map/all_to_all | solution.py:107
  61.2 32.3 %all-to-all-start.1 = ((bf16[16,384,3]{1,2,0:T(4,128)(2,1)}), bf16[16,384,3]{1,2,0:T(4,128)(2,1)S(1)}, u32[]{:S(2)}, u32[]{:S(2)}) async-start(bf16[16,384,3]{1,2,0:T(4,128)(2,1)} %bitcast.2), calls=%async_computation.1 | async-start | bytes 98304 | tf_op jit(solution)/shard_map/all_to_all | solution.py:146
  81.5 19.1 %copy-start.3 = (f32[48]{0:T(128)S(1)}, f32[48]{0:T(128)}, u32[]{:S(2)}) copy-start(f32[48]{0:T(128)} %param.22) | copy-start | bytes 580
  93.5 13.7 %all-to-all-start.2 = ((bf16[12,16,192]{2,0,1:T(8,128)(2,1)}), bf16[12,16,192]{2,0,1:T(8,128)(2,1)S(1)}, u32[]{:S(2)}, u32[]{:S(2)}) async-start(bf16[12,16,192]{2,0,1:T(8,128)(2,1)} %copy.156), calls=%async_computation.2 | async-start | bytes 262144 | tf_op jit(solution)/shard_map/all_to_all | solution.py:104
  107.2 18.5 %all-to-all-start.6 = ((bf16[12,16,192]{2,0,1:T(8,128)(2,1)}), bf16[12,16,192]{2,0,1:T(8,128)(2,1)S(1)}, u32[]{:S(2)}, u32[]{:S(2)}) async-start(bf16[12,16,192]{2,0,1:T(8,128)(2,1)} %copy.174), calls=%async_computation.6 | async-start | bytes 262144 | tf_op jit(solution)/shard_map/all_to_all | solution.py:101
  125.8 19.3 %all-to-all-start.5 = ((bf16[16,384,16]{1,2,0:T(8,128)(2,1)}), bf16[16,384,16]{1,2,0:T(8,128)(2,1)S(1)}, u32[]{:S(2)}, u32[]{:S(2)}) async-start(bf16[16,384,16]{1,2,0:T(8,128)(2,1)} %bitcast.216), calls=%async_computation.5 | async-start | bytes 393216 | tf_op jit(solution)/shard_map/all_to_all | solution.py:145
  145.1 50.6 %all-to-all-start.3 = ((bf16[16,384,192]{1,2,0:T(8,128)(2,1)}), bf16[16,384,192]{1,2,0:T(8,128)(2,1)}, u32[]{:S(2)}, u32[]{:S(2)}) async-start(bf16[16,384,192]{1,2,0:T(8,128)(2,1)} %bitcast.253), calls=%async_computation.3 | async-start | bytes 4718592 | tf_op jit(solution)/shard_map/all_to_all | solution.py:144
  195.7 206.0 %all-to-all-start.7 = ((bf16[16,384,192]{1,2,0:T(8,128)(2,1)}), bf16[16,384,192]{1,2,0:T(8,128)(2,1)}, u32[]{:S(2)}, u32[]{:S(2)}) async-start(bf16[16,384,192]{1,2,0:T(8,128)(2,1)} %bitcast.252), calls=%async_computation.7 | async-start | bytes 4718592 | tf_op jit(solution)/shard_map/all_to_all | solution.py:143
  202.6 2.1 copy-start.1
  392.6 9.1 %copy-start = (f32[1,48,64,128]{3,2,1,0:T(8,128)}, f32[1,48,64,128]{3,2,1,0:T(8,128)S(1)}, u32[]{:S(2)}) copy-start(f32[1,48,64,128]{3,2,1,0:T(8,128)S(1)} %get-tuple-element.59) | copy-start | bytes 4718596
  401.7 33.3 %all-to-all-start.9 = ((bf16[12,16,192]{2,0,1:T(8,128)(2,1)}), bf16[12,16,192]{2,0,1:T(8,128)(2,1)S(1)}, u32[]{:S(2)}, u32[]{:S(2)}) async-start(bf16[12,16,192]{2,0,1:T(8,128)(2,1)} %copy.176), calls=%async_computation.9 | async-start | bytes 262144 | tf_op jit(solution)/shard_map/all_to_all | solution.py:113
  408.3 15.3 %copy-start.2 = (f32[3072]{0:T(1024)S(1)}, f32[3072]{0:T(1024)}, u32[]{:S(2)}) copy-start(f32[3072]{0:T(1024)} %param.25) | copy-start | bytes 36868
  435.0 34.5 %all-to-all-start.8 = ((bf16[16,1,384,192]{2,3,1,0:T(8,128)(2,1)}), bf16[16,1,384,192]{2,3,1,0:T(8,128)(2,1)}, u32[]{:S(2)}, u32[]{:S(2)}) async-start(bf16[16,1,384,192]{2,3,1,0:T(8,128)(2,1)} %fusion.59), calls=%async_computation.8 | async-start | bytes 4718592 | tf_op jit(solution)/shard_map/all_to_all | solution.py:166
  441.7 264.0 %reduce-scatter.4.cloned.1.call-start = ((), (), s32[]{:S(2)}) async-start(), calls=%async_computation.11 | async-start | bytes 40108032
Sparse Core Ops, SparseCore 0:
  486.1 219.4 reduce-scatter.3
